TPU v7x, 32 devices: a whole 2x2x4 slice. The times are simulated.
32 devices in a mesh: subtree: 8 (over z, core), front: 4 (over y, x).
Axes of the slice: x: 2, y: 2, z: 4, core: 2. Of those that a mesh axis runs over, the one named last changes fastest.
Arguments:
- leaf_rhs: float32 [8, 2048, 256], P('subtree', 'front'), may hold values from -6 to 6
- mid_rhs: float32 [2, 4096, 256], P(None, 'front'), may hold values from -6 to 6
- root_rhs: float32 [10240, 256], P('front'), may hold values from -6 to 6
- leaf_lower: float32 [8, 2048, 2048], P('subtree', None, 'front'), may hold values from -0.125 to 0.125
- leaf_below: float32 [8, 2048, 2048], P('subtree', None, 'front'), may hold values from -0.125 to 0.125
- leaf_right: float32 [8, 2048, 2048], P('subtree', None, 'front'), may hold values from -0.125 to 0.125
- leaf_upper: float32 [8, 2048, 2048], P('subtree', None, 'front'), may hold values from -0.125 to 0.125
- mid_lower: float32 [2, 4096, 4096], P(None, 'subtree', 'front'), may hold values from -0.09375 to 0.09375
- mid_below: float32 [2, 4096, 4096], P(None, 'front', 'subtree'), may hold values from -0.09375 to 0.09375
- mid_right: float32 [2, 4096, 4096], P(None, 'subtree', 'front'), may hold values from -0.09375 to 0.09375
- mid_upper: float32 [2, 4096, 4096], P(None, 'front', 'subtree'), may hold values from -0.09375 to 0.09375
- root_lower: float32 [10240, 10240], P('subtree', 'front'), may hold values from -0.0625 to 0.0625
- root_upper: float32 [10240, 10240], P('front', 'subtree'), may hold values from -0.0625 to 0.0625
- leaf_parent: int32 [8], replicated, may hold values from 0 to 1, as said below
- leaf_sizes: int32 [8], replicated, may hold values from 1024 to 2048, as said below
- leaf_map: int32 [8, 16], replicated, may hold values from 0 to 63, as said below
- mid_map: int32 [2, 32], replicated, may hold values from 0 to 79, as said below
Outputs:
- leaf_sol: float32 [8, 2048, 256], P('subtree', 'front')
- mid_sol: float32 [2, 4096, 256], P(None, 'front')
- root_sol: float32 [10240, 256], P('front')
Inputs may be any that keep to these rules, and one draw needn't show every extreme that they name: `leaf_parent`: every level-1 front is the parent of at least one lowest-level front. `leaf_sizes`: a multiple of 128; some front has all 2048 rows live. `leaf_map`: a front's blocks go to distinct parent blocks; update block b of a lowest-level front, with c = b // 4, goes to c * 8 + i or to that plus 4096 / 128, for some i with 0 <= i < 8. `mid_map`: a front's blocks go to distinct root blocks; update block b of a level-1 front, with c = b // 8, goes to c * 20 + i for some i with 0 <= i < 20.
All inputs are finite; a program needn't handle non-finite values.
Results may differ from a plain program's by a relative error of at most 0.00013.
Values sent between devices are 32-bit elements; how exact they have to be, the bound alone decides.
No kernel may reach another device: no remote copies, remote signals or barrier semaphores. Data moves between devices by JAX's collectives and lax.ppermute only.
A program may use at most 128 MiB of HBM per device.

v0:
```python
import jax
import jax.numpy as jnp
from jax import lax
from jax.sharding import PartitionSpec as P

MID_PIV = 4096
BLOCK = 128


def leaf_product(matrix, vector):
    return lax.psum_scatter(
        jnp.dot(
            matrix, vector, preferred_element_type=jnp.float32, precision=lax.Precision.HIGHEST
        ),
        "front",
        scatter_dimension=0,
        tiled=True,
    )


def across_front(partial_value):
    return lax.psum(partial_value, "front")


def across_subtree(partial_value):
    return lax.psum(partial_value, "subtree")


def batched(matrix, vector):
    return jnp.einsum(
        "fab,fbr->far",
        matrix,
        vector,
        preferred_element_type=jnp.float32,
        precision=lax.Precision.HIGHEST,
    )


def leaf_select(parents, blocks, fronts, column, width):
    front_ids = jnp.arange(fronts, dtype=jnp.int32)[:, None, None, None, None]
    halves = jnp.arange(2, dtype=jnp.int32)[None, :, None, None, None]
    slots = jnp.arange(width, dtype=jnp.int32)[None, None, :, None, None]
    target = halves * (MID_PIV // BLOCK) + column * width + slots
    match_parent = parents[None, None, None, :, None] == front_ids
    match_block = blocks[None, None, None, :, :] == target
    return (match_parent & match_block).astype(jnp.float32)


def on_device(
    leaf_rhs,
    mid_rhs,
    root_rhs,
    leaf_lower,
    leaf_below,
    leaf_right,
    leaf_upper,
    mid_lower,
    mid_below,
    mid_right,
    mid_upper,
    root_lower,
    root_upper,
    leaf_parent,
    leaf_sizes,
    leaf_map,
    mid_map,
):
    group = lax.axis_index("subtree")
    column = lax.axis_index("front")
    local_rows = leaf_rhs.shape[1]
    scenarios = leaf_rhs.shape[2]
    leaf_width = local_rows // BLOCK
    fronts = mid_rhs.shape[0]
    mid_width = mid_rhs.shape[1] // BLOCK
    root_width = root_rhs.shape[0] // BLOCK
    own_size = lax.dynamic_slice_in_dim(leaf_sizes, group, 1)
    positions = column * local_rows + jnp.arange(local_rows, dtype=jnp.int32)
    live = (positions < own_size[0]).astype(jnp.float32)[:, None]
    leaf_fwd = live * leaf_product(leaf_lower[0], live * leaf_rhs[0])
    leaf_contrib = -leaf_product(leaf_below[0], leaf_fwd)
    own_parent = lax.dynamic_slice_in_dim(leaf_parent, group, 1)
    own_blocks = lax.dynamic_slice(leaf_map, (group, column * leaf_width), (1, leaf_width))
    own_select = leaf_select(own_parent, own_blocks, fronts, column, mid_width)
    column_blocks = lax.dynamic_slice_in_dim(leaf_map, column * leaf_width, leaf_width, 1)
    selection = leaf_select(leaf_parent, column_blocks, fronts, column, mid_width)
    piece = lax.all_gather(leaf_contrib[None], "subtree", axis=0, tiled=True)
    shaped = piece.reshape(piece.shape[0], leaf_width, BLOCK, scenarios)
    assembled = jnp.einsum(
        "phqgk,gkbr->phqbr",
        selection,
        shaped,
        preferred_element_type=jnp.float32,
        precision=lax.Precision.HIGHEST,
    )
    mid_pivot = mid_rhs + assembled[:, 0].reshape(fronts, mid_width * BLOCK, scenarios)
    mid_update = assembled[:, 1].reshape(fronts, mid_width * BLOCK, scenarios)
    mid_fwd = across_front(batched(mid_lower, mid_pivot))
    mid_contrib = mid_update - across_subtree(batched(mid_below, mid_fwd))
    column_map = lax.dynamic_slice_in_dim(mid_map, column * mid_width, mid_width, 1)
    slots = jnp.arange(root_width, dtype=jnp.int32)[:, None, None]
    root_select = (column_map[None, :, :] == column * root_width + slots).astype(jnp.float32)
    root_added = jnp.einsum(
        "qpk,pkbr->qbr",
        root_select,
        mid_contrib.reshape(fronts, mid_width, BLOCK, scenarios),
        preferred_element_type=jnp.float32,
        precision=lax.Precision.HIGHEST,
    )
    root_start = root_rhs + root_added.reshape(root_width * BLOCK, scenarios)
    root_fwd = across_front(
        jnp.dot(
            root_lower,
            root_start,
            preferred_element_type=jnp.float32,
            precision=lax.Precision.HIGHEST,
        )
    )
    root_sol = across_subtree(
        jnp.dot(
            root_upper,
            root_fwd,
            preferred_element_type=jnp.float32,
            precision=lax.Precision.HIGHEST,
        )
    )
    mid_ext = jnp.einsum(
        "qpk,qbr->pkbr",
        root_select,
        root_sol.reshape(root_width, BLOCK, scenarios),
        preferred_element_type=jnp.float32,
        precision=lax.Precision.HIGHEST,
    )
    mid_ext = mid_ext.reshape(fronts, mid_width * BLOCK, scenarios)
    mid_back = mid_fwd - across_front(batched(mid_right, mid_ext))
    mid_sol = across_subtree(batched(mid_upper, mid_back))
    whole_column = jnp.stack(
        [
            mid_sol.reshape(fronts, mid_width, BLOCK, scenarios),
            mid_ext.reshape(fronts, mid_width, BLOCK, scenarios),
        ],
        axis=1,
    )
    leaf_ext = jnp.einsum(
        "phqgk,phqbr->gkbr",
        own_select,
        whole_column,
        preferred_element_type=jnp.float32,
        precision=lax.Precision.HIGHEST,
    )
    leaf_ext = leaf_ext.reshape(local_rows, scenarios)
    leaf_back = live * (leaf_fwd - leaf_product(leaf_right[0], leaf_ext))
    leaf_sol = live * leaf_product(leaf_upper[0], leaf_back)
    return (leaf_sol[None], mid_sol, root_sol)


def solution(mesh):
    return jax.shard_map(
        on_device,
        mesh=mesh,
        in_specs=(
            P("subtree", "front", None),
            P(None, "front", None),
            P("front", None),
            P("subtree", None, "front"),
            P("subtree", None, "front"),
            P("subtree", None, "front"),
            P("subtree", None, "front"),
            P(None, "subtree", "front"),
            P(None, "front", "subtree"),
            P(None, "subtree", "front"),
            P(None, "front", "subtree"),
            P("subtree", "front"),
            P("front", "subtree"),
            P(),
            P(),
            P(),
            P(),
        ),
        out_specs=(P("subtree", "front", None), P(None, "front", None), P("front", None)),
        check_vma=False,
    )
```

profile of v0, /device:TPU:0, one launch (start us, length us, event | category | flops | bytes accessed | tf_op | source)
XLA Modules:
  0.0 725.7 jit_solution(1965828273986753131)
XLA Ops:
  7.2 1.2 dynamic_slice.15
  8.5 0.6 fusion.57
  9.1 10.6 %fusion.15 = f32[2048,256]{0,1:T(8,128)} fusion(f32[1,2048,512]{2,1,0:T(8,128)} %param.20, f32[1,512,256]{2,1,0:T(8,128)} %param.17, f32[512]{0:T(512)S(1)} %fusion.57), kind=kOutput, calls=%fused_computation.16 | convolution fusion | flops 3221356544 | bytes 6817792 | tf_op jit(solution)/shard_map/dot_general | solution.py:12
  19.8 38.0 %reduce-scatter.5.cloned.1.call-done = f32[512,256]{0,1:T(8,128)} async-done(((f32[2048,256]{0,1:T(8,128)}), f32[512,256]{0,1:T(8,128)}) %reduce-scatter.5.cloned.1.call-update) | async-done | bytes 524304 | tf_op jit(solution)/shard_map/reduce_scatter | solution.py:11
  57.8 7.3 %fusion.18 = f32[2048,256]{0,1:T(8,128)} fusion(f32[1,2048,512]{2,1,0:T(8,128)} %param.21, f32[512,256]{0,1:T(8,128)} %reduce-scatter.5.cloned.1.call-done, f32[512]{0:T(512)S(1)} %fusion.57), kind=kOutput, calls=%fused_computation.17 | convolution fusion | flops 3221356544 | bytes 6817792 | tf_op jit(solution)/shard_map/dot_general | solution.py:12
  65.2 35.3 %reduce-scatter.7.cloned.1.call-done = f32[512,256]{0,1:T(8,128)} async-done(((f32[2048,256]{0,1:T(8,128)}), f32[512,256]{0,1:T(8,128)}) %reduce-scatter.7.cloned.1.call-update) | async-done | bytes 524304 | tf_op jit(solution)/shard_map/reduce_scatter | solution.py:11
  100.5 1.9 neg.3
  102.4 0.2 all-reduce.7.cloned.1.call-start
  102.6 0.1 constant_dynamic-slice_fusion.1
  102.7 0.1 copy.29
  102.8 0.1 iota_add_fusion
  102.8 0.1 broadcast_compare_fusion
  102.9 46.6 %all-gather.3.cloned.1.call-done = f32[4096,256]{0,1:T(8,128)} async-done(((f32[512,256]{0,1:T(8,128)}), f32[4096,256]{0,1:T(8,128)}) %all-gather.3.cloned.1.call-update) | async-done | bytes 4194320 | tf_op jit(solution)/shard_map/all_gather | solution.py:86
  149.5 6.0 reshape.127
  155.6 6.6 copy.48
  162.2 6.1 convolution_bitcast_fusion.2
  168.3 0.4 fusion.59
  168.6 0.6 copy.31
  169.3 0.6 copy-done.6
  169.8 1.3 copy-done.2
  171.2 8.0 %fusion.29 = f32[2,512,256]{1,2,0:T(8,128)} fusion(f32[2,512,1024]{2,1,0:T(8,128)S(1)} %copy-done.2, f32[2,1024,256]{2,1,0:T(8,128)S(1)} %copy-done.6, f32[2,1024,256]{2,1,0:T(8,128)S(1)} %bitcast.122), kind=kOutput, calls=%fused_computation.28 | convolution fusion | flops 3221749760 | bytes 9437184 | tf_op jit(solution)/shard_map/fab,fbr->far/dot_general | solution.py:30
  179.2 0.3 all-reduce.9.cloned.1.call-start
  179.4 51.2 %all-reduce.7.cloned.1.call-done = f32[2,512,256]{1,2,0:T(8,128)} async-done(((f32[2,512,256]{1,2,0:T(8,128)}), f32[2,512,256]{1,2,0:T(8,128)}) %all-reduce.7.cloned.1.call-update) | async-done | bytes 1048592 | tf_op jit(solution)/shard_map/psum | solution.py:22
  230.6 7.5 %convolution_bitcast_fusion.5 = f32[2,1024,256]{1,2,0:T(8,128)} fusion(f32[2,512,256]{1,2,0:T(8,128)} %all-reduce.7.cloned.1.call-done, f32[2,1024,512]{2,1,0:T(8,128)} %param.25), kind=kOutput, calls=%fused_computation.27 | convolution fusion | flops 3221225472 | bytes 7340032 | tf_op jit(solution)/shard_map/fab,fbr->far/dot_general | solution.py:30
  238.2 0.1 constant_dynamic-slice_fusion
  238.3 1.9 copy.33
  240.2 1.9 copy.34
  242.1 61.3 %all-reduce.9.cloned.1.call-done = f32[2,1024,256]{1,2,0:T(8,128)} async-done(((f32[2,1024,256]{1,2,0:T(8,128)}), f32[2,1024,256]{1,2,0:T(8,128)}) %all-reduce.9.cloned.1.call-update) | async-done | bytes 2097168 | tf_op jit(solution)/shard_map/psum | solution.py:26
  303.4 2.1 sub.9
  305.5 0.5 copy.59
  305.9 2.0 copy.35
  308.0 3.2 convolution_bitcast_fusion.3
  311.2 0.8 copy.36
  312.0 0.9 copy-done.5
  312.9 0.3 bitcast_add_fusion
  313.2 26.2 %convolution_bitcast_fusion.1 = f32[1280,256]{0,1:T(8,128)} fusion(f32[2560,256]{1,0:T(8,128)S(1)} %bitcast_add_fusion, f32[1280,2560]{1,0:T(8,128)} %param.28), kind=kOutput, calls=%fused_computation.20 | convolution fusion | flops 10066329600 | bytes 17039360 | tf_op jit(solution)/shard_map/dot_general | solution.py:111
  339.5 56.1 %all-reduce.11.cloned.1.call-done = f32[1280,256]{0,1:T(8,128)} async-done(((f32[1280,256]{0,1:T(8,128)}), f32[1280,256]{0,1:T(8,128)}) %all-reduce.11.cloned.1.call-update) | async-done | bytes 1310736 | tf_op jit(solution)/shard_map/psum | solution.py:22
  395.6 15.6 %convolution_bitcast_fusion = f32[2560,256]{0,1:T(8,128)} fusion(f32[1280,256]{0,1:T(8,128)} %all-reduce.11.cloned.1.call-done, f32[2560,1280]{1,0:T(8,128)} %param.29), kind=kOutput, calls=%fused_computation.12 | convolution fusion | flops 10066329600 | bytes 17039360 | tf_op jit(solution)/shard_map/dot_general | solution.py:119
  411.3 69.2 %all-reduce.13.cloned.1.call-done = f32[2560,256]{0,1:T(8,128)} async-done(((f32[2560,256]{0,1:T(8,128)}), f32[2560,256]{0,1:T(8,128)}) %all-reduce.13.cloned.1.call-update) | async-done | bytes 2621456 | tf_op jit(solution)/shard_map/psum | solution.py:26
  480.5 3.2 copy.37
  483.7 4.4 fusion.12
  488.1 0.6 copy.39
  488.7 1.5 copy-done.1
  490.3 8.0 %convolution_bitcast_fusion.6 = f32[2,512,256]{1,2,0:T(8,128)} fusion(f32[2,1024,256]{2,1,0:T(8,128)S(1)} %bitcast.118, f32[2,512,1024]{2,1,0:T(8,128)S(1)} %copy-done.1), kind=kOutput, calls=%fused_computation.29 | convolution fusion | flops 3221225472 | bytes 7340032 | tf_op jit(solution)/shard_map/fab,fbr->far/dot_general | solution.py:30
  498.3 0.3 all-reduce.17.cloned.1.call-start
  498.6 51.4 %all-reduce.15.cloned.1.call-done = f32[2,512,256]{1,2,0:T(8,128)} async-done(((f32[2,512,256]{1,2,0:T(8,128)}), f32[2,512,256]{1,2,0:T(8,128)}) %all-reduce.15.cloned.1.call-update) | async-done | bytes 1048592 | tf_op jit(solution)/shard_map/psum | solution.py:22
  550.0 7.5 %convolution_bitcast_fusion.4 = f32[2,1024,256]{1,2,0:T(8,128)} fusion(f32[2,1024,512]{2,1,0:T(8,128)} %param.27, f32[2,512,256]{1,2,0:T(8,128)S(1)} %copy-done.4, f32[2,512,256]{1,2,0:T(8,128)} %all-reduce.15.cloned.1.call-done), kind=kOutput, calls=%fused_computation.26 | convolution fusion | flops 3221487616 | bytes 8388608 | tf_op jit(solution)/shard_map/fab,fbr->far/dot_general | solution.py:30
  557.6 0.6 dynamic_slice.16
  558.2 0.1 dynamic-slice_bitcast_fusion
  558.2 0.6 iota_compare_fusion.1
  558.9 0.1 broadcast_compare_fusion.1
  559.0 63.8 %all-reduce.17.cloned.1.call-done = f32[2,1024,256]{1,2,0:T(8,128)} async-done(((f32[2,1024,256]{1,2,0:T(8,128)}), f32[2,1024,256]{1,2,0:T(8,128)}) %all-reduce.17.cloned.1.call-update) | async-done | bytes 2097168 | tf_op jit(solution)/shard_map/psum | solution.py:26
  622.8 2.9 copy.40
  625.6 2.8 copy.41
  628.5 1.9 fusion.32
  630.4 0.1 copy.43
  630.5 0.1 copy-done.3
  630.6 8.4 %fusion.21 = f32[2048,256]{0,1:T(8,128)} fusion(f32[512,256]{1,0:T(8,128)S(1)} %bitcast.123, f32[1,2048,512]{2,1,0:T(8,128)S(1)} %copy-done.3), kind=kOutput, calls=%fused_computation.18 | convolution fusion | flops 3221225472 | bytes 6815744 | tf_op jit(solution)/shard_map/dot_general | solution.py:12
  639.0 0.3 reduce-scatter.11.cloned.1.call-start
  639.3 34.6 %reduce-scatter.9.cloned.1.call-done = f32[512,256]{0,1:T(8,128)} async-done(((f32[2048,256]{0,1:T(8,128)}), f32[512,256]{0,1:T(8,128)}) %reduce-scatter.9.cloned.1.call-update) | async-done | bytes 524304 | tf_op jit(solution)/shard_map/reduce_scatter | solution.py:11
  674.0 7.4 %fusion.24 = f32[2048,256]{0,1:T(8,128)} fusion(f32[1,2048,512]{2,1,0:T(8,128)} %param.23, f32[512,256]{0,1:T(8,128)} %reduce-scatter.9.cloned.1.call-done, f32[512,256]{0,1:T(8,128)S(1)} %copy-done.7, f32[512]{0:T(512)S(1)} %fusion.57), kind=kOutput, calls=%fused_computation.19 | convolution fusion | flops 3221618688 | bytes 7342080 | tf_op jit(solution)/shard_map/dot_general | solution.py:12
  681.3 35.3 %reduce-scatter.11.cloned.1.call-done = f32[512,256]{0,1:T(8,128)} async-done(((f32[2048,256]{0,1:T(8,128)}), f32[512,256]{0,1:T(8,128)}) %reduce-scatter.11.cloned.1.call-update) | async-done | bytes 524304 | tf_op jit(solution)/shard_map/reduce_scatter | solution.py:11
  716.7 1.1 multiply_bitcast_fusion
  717.8 1.0 copy.44
  (36 shorter events, 0.5 us)
Async XLA Ops:
  7.2 95.4 %copy-start = (s32[8,16]{1,0:T(8,128)S(1)}, s32[8,16]{1,0:T(8,128)}, u32[]{:S(2)}) copy-start(s32[8,16]{1,0:T(8,128)} %param.32) | copy-start | bytes 1540
  7.2 50.6 %reduce-scatter.5.cloned.1.call-start = ((), (), s32[]{:S(2)}) async-start(), calls=%async_computation.4 | async-start | bytes 2621440 | tf_op jit(solution)/shard_map/reduce_scatter | solution.py:11
  19.7 80.7 %reduce-scatter.7.cloned.1.call-start = ((), (), s32[]{:S(2)}) async-start(), calls=%async_computation.5 | async-start | bytes 2621440 | tf_op jit(solution)/shard_map/reduce_scatter | solution.py:11
  65.1 37.7 %copy-start.9 = (s32[8]{0:T(128)S(1)}, s32[8]{0:T(128)}, u32[]{:S(2)}) copy-start(s32[8]{0:T(128)} %param.30) | copy-start | bytes 100
  65.1 84.4 %all-gather.3.cloned.1.call-start = ((), (), s32[]{:S(2)}) async-start(), calls=%async_computation.14 | async-start | bytes 4718592 | tf_op jit(solution)/shard_map/all_gather | solution.py:86
  102.4 128.2 %all-reduce.7.cloned.1.call-start = ((), (), s32[]{:S(2)}) async-start(), calls=%async_computation.6 | async-start | bytes 2097152 | tf_op jit(solution)/shard_map/psum | solution.py:22
  168.3 1.6 copy-start.6
  168.6 2.5 copy-start.2
  179.2 59.0 %copy-start.8 = (s32[2,32]{1,0:T(2,128)S(1)}, s32[2,32]{1,0:T(2,128)}, u32[]{:S(2)}) copy-start(s32[2,32]{1,0:T(2,128)} %param.33) | copy-start | bytes 772
  179.2 124.2 %all-reduce.9.cloned.1.call-start = ((), (), s32[]{:S(2)}) async-start(), calls=%async_computation.7 | async-start | bytes 4194304 | tf_op jit(solution)/shard_map/psum | solution.py:26
  238.1 157.4 %all-reduce.11.cloned.1.call-start = ((), (), s32[]{:S(2)}) async-start(), calls=%async_computation.8 | async-start | bytes 2621440 | tf_op jit(solution)/shard_map/psum | solution.py:22
  311.2 1.7 copy-start.5
  339.4 141.1 %all-reduce.13.cloned.1.call-start = ((), (), s32[]{:S(2)}) async-start(), calls=%async_computation.9 | async-start | bytes 5242880 | tf_op jit(solution)/shard_map/psum | solution.py:26
  411.2 138.8 %all-reduce.15.cloned.1.call-start = ((), (), s32[]{:S(2)}) async-start(), calls=%async_computation.10 | async-start | bytes 2097152 | tf_op jit(solution)/shard_map/psum | solution.py:22
  488.1 2.2 copy-start.1
  490.3 59.8 %copy-start.4 = (f32[2,512,256]{1,2,0:T(8,128)S(1)}, f32[2,512,256]{1,2,0:T(8,128)}, u32[]{:S(2)}) copy-start(f32[2,512,256]{1,2,0:T(8,128)} %all-reduce.7.cloned.1.call-done) | copy-start | bytes 3145732
  498.3 124.4 %all-reduce.17.cloned.1.call-start = ((), (), s32[]{:S(2)}) async-start(), calls=%async_computation.11 | async-start | bytes 4194304 | tf_op jit(solution)/shard_map/psum | solution.py:26
  557.5 116.4 %reduce-scatter.9.cloned.1.call-start = ((), (), s32[]{:S(2)}) async-start(), calls=%async_computation.12 | async-start | bytes 2621440 | tf_op jit(solution)/shard_map/reduce_scatter | solution.py:11
  628.5 2.2 copy-start.3
  630.6 43.3 %copy-start.7 = (f32[512,256]{0,1:T(8,128)S(1)}, f32[512,256]{0,1:T(8,128)}, u32[]{:S(2)}) copy-start(f32[512,256]{0,1:T(8,128)} %reduce-scatter.5.cloned.1.call-done) | copy-start | bytes 1572868
  639.0 77.7 %reduce-scatter.11.cloned.1.call-start = ((), (), s32[]{:S(2)}) async-start(), calls=%async_computation.13 | async-start | bytes 2621440 | tf_op jit(solution)/shard_map/reduce_scatter | solution.py:11
Sparse Core Ops, SparseCore 0:
  19.8 37.9 reduce-scatter.4
  65.2 35.1 reduce-scatter.6
  102.6 46.8 all-gather.2
  179.3 51.2 all-reduce.6
  238.2 65.1 all-reduce.8
  339.6 55.9 all-reduce.10
  411.3 69.0 all-reduce.12
  498.4 51.5 all-reduce.14
  557.6 65.0 all-reduce.16
  639.1 34.7 reduce-scatter.8
  681.5 35.1 reduce-scatter.10
where the time goes:
time: 734 us; the launch traced here: 726 us
  waiting for transfers between devices  543 us (74%)
  matrix products  122 us (17%)
  local copies, waits for them, and re-layouts  38.1 us (5%)
  between operations  14.5 us (2%)
    psum x3, waiting for transfers between devices, across_subtree(): return lax.psum(partial_value, 'subtree')  194 us
    psum x3, waiting for transfers between devices, across_front(): return lax.psum(partial_value, 'front')  159 us
    reduce_scatter x4, waiting for transfers between devices, leaf_product(): lax.psum_scatter(jnp.dot(matrix, vector, preferred_element_type=jnp.float...  143 us
    all_gather x1, waiting for transfers between devices, on_device(): piece = lax.all_gather(leaf_contrib[None], 'subtree', axis=0, tiled=True)  46.6 us
    dot_general x4, matrix products, leaf_product(): jnp.dot(matrix, vector, preferred_element_type=jnp.float32, precision=lax...  33.6 us
    dot_general x4, matrix products, batched(): jnp.einsum('fab,fbr->far', matrix, vector, preferred_element_type=jnp.flo...  31 us
    dot_general x1, matrix products, on_device(): jnp.dot(root_lower, root_start, preferred_element_type=jnp.float32, preci...  26.2 us
    dot_general x1, matrix products, on_device(): jnp.dot(root_upper, root_fwd, preferred_element_type=jnp.float32, precisi...  15.6 us
  transfers between devices with their start and end apart: 11, of which 11 were waited for; matrix products, arithmetic and copies ran while one was open for 1% of the time, Pallas kernels for 0%

commit v1 on v0

--- a/solution.py
+++ b/solution.py
@@ -5,6 +5,11 @@
 
 MID_PIV = 4096
 BLOCK = 128
+
+
+def gather_and_add(shard, axis):
+    shards = lax.all_gather(shard, axis)
+    return jnp.sum(shards, axis=0)
 
 
 def leaf_product(matrix, vector):
@@ -23,7 +28,7 @@
 
 
 def across_subtree(partial_value):
-    return lax.psum(partial_value, "subtree")
+    return gather_and_add(partial_value, "subtree")
 
 
 def batched(matrix, vector):

time: 734 us -> 1060 us (1.44)
  waiting for transfers between devices: 543 us -> 832 us
  other arithmetic: 6.88 us -> 27.6 us
  local copies, waits for them, and re-layouts: 38.1 us -> 57.4 us
    all_gather x0 -> x3, waiting for transfers between devices: none -> 486 us  [gather_and_add(): shards = lax.all_gather(shard, axis)]
    psum x3 -> x0, waiting for transfers between devices: 194 us -> none  [across_subtree(): return lax.psum(partial_value, 'subtree')]
    unnamed x22 -> x24, local copies, waits for them, and re-layouts: 5.98 us -> 30.5 us
    reduce_sum x0 -> x3, other arithmetic: none -> 22.8 us  [gather_and_add(): return jnp.sum(shards, axis=0)]
  transfers between devices with their start and end apart: 11 -> 11, of which waited for: 11 -> 11; matrix products, arithmetic and copies ran while one was open for 1% -> 0% of each run, Pallas kernels for 0% -> 0%
where the time goes in v1:
time: 1060 us; the launch traced here: 1050 us
  waiting for transfers between devices  832 us (78%)
  matrix products  122 us (12%)
  local copies, waits for them, and re-layouts  57.4 us (5%)
  other arithmetic  27.6 us (3%)
  between operations  14.5 us (1%)
    all_gather x3, waiting for transfers between devices, gather_and_add(): shards = lax.all_gather(shard, axis)  486 us
    psum x3, waiting for transfers between devices, across_front(): return lax.psum(partial_value, 'front')  157 us
    reduce_scatter x4, waiting for transfers between devices, leaf_product(): lax.psum_scatter(jnp.dot(matrix, vector, preferred_element_type=jnp.float...  142 us
    all_gather x1, waiting for transfers between devices, on_device(): piece = lax.all_gather(leaf_contrib[None], 'subtree', axis=0, tiled=True)  46.6 us
    dot_general x4, matrix products, leaf_product(): jnp.dot(matrix, vector, preferred_element_type=jnp.float32, precision=lax...  33.6 us
    unnamed x24, local copies, waits for them, and re-layouts  30.5 us
    dot_general x4, matrix products, batched(): jnp.einsum('fab,fbr->far', matrix, vector, preferred_element_type=jnp.flo...  29.9 us
    dot_general x1, matrix products, on_device(): jnp.dot(root_lower, root_start, preferred_element_type=jnp.float32, preci...  25.9 us
  transfers between devices with their start and end apart: 11, of which 11 were waited for; matrix products, arithmetic and copies ran while one was open for 0% of the time, Pallas kernels for 0%

profile of v1, /device:TPU:0, one launch (start us, length us, event | category | flops | bytes accessed | tf_op | source)
XLA Modules:
  0.0 1054.3 jit_solution(7817309470348441923)
XLA Ops:
  7.2 1.2 dynamic_slice.15
  8.5 0.6 fusion.68
  9.1 10.5 fusion.15
  19.7 38.0 %reduce-scatter.5.cloned.1.call-done = f32[512,256]{0,1:T(8,128)} async-done(((f32[2048,256]{0,1:T(8,128)}), f32[512,256]{0,1:T(8,128)}) %reduce-scatter.5.cloned.1.call-update) | async-done | bytes 524304 | tf_op jit(solution)/shard_map/reduce_scatter | solution.py:16
  57.8 7.3 fusion.18
  65.2 35.3 %reduce-scatter.7.cloned.1.call-done = f32[512,256]{0,1:T(8,128)} async-done(((f32[2048,256]{0,1:T(8,128)}), f32[512,256]{0,1:T(8,128)}) %reduce-scatter.7.cloned.1.call-update) | async-done | bytes 524304 | tf_op jit(solution)/shard_map/reduce_scatter | solution.py:16
  100.4 1.9 neg.3
  102.3 0.3 all-reduce.4.cloned.1.call-start
  102.6 0.1 constant_dynamic-slice_fusion.1
  102.7 0.1 copy.62
  102.8 0.1 iota_add_fusion
  102.9 0.1 broadcast_compare_fusion
  102.9 46.6 %all-gather.9.cloned.1.call-done = f32[4096,256]{0,1:T(8,128)} async-done(((f32[512,256]{0,1:T(8,128)}), f32[4096,256]{0,1:T(8,128)}) %all-gather.9.cloned.1.call-update) | async-done | bytes 4194320 | tf_op jit(solution)/shard_map/all_gather | solution.py:91
  149.5 6.0 reshape.127
  155.5 6.6 copy.86
  162.1 6.0 convolution_bitcast_fusion.2
  168.2 0.1 slice.8
  168.4 0.6 copy.64
  169.0 1.3 copy-done.1
  170.3 1.0 copy-done.7
  171.3 1.2 copy-done.3
  172.5 7.8 fusion.36
  180.4 51.4 %all-reduce.4.cloned.1.call-done = f32[2,512,256]{1,2,0:T(8,128)} async-done(((f32[2,512,256]{1,2,0:T(8,128)}), f32[2,512,256]{1,2,0:T(8,128)}) %all-reduce.4.cloned.1.call-update) | async-done | bytes 1048592 | tf_op jit(solution)/shard_map/psum | solution.py:27
  231.8 6.6 convolution_bitcast_fusion.4
  238.4 1.8 copy.66
  240.3 0.1 constant_dynamic-slice_fusion
  240.4 151.1 %all-gather.11.cloned.1.call-done = f32[16,1024,256]{2,1,0:T(8,128)} async-done(((f32[2,1024,256]{2,1,0:T(8,128)}), f32[16,1024,256]{2,1,0:T(8,128)}) %all-gather.11.cloned.1.call-update) | async-done | bytes 16777232 | tf_op jit(solution)/shard_map/all_gather | solution.py:11
  391.5 7.3 reduce_sum.29
  398.7 4.3 fusion.33
  403.1 0.8 copy.71
  403.9 0.9 copy-done.6
  404.8 0.3 bitcast_add_fusion
  405.1 25.9 %convolution_bitcast_fusion.1 = f32[1280,256]{0,1:T(8,128)} fusion(f32[2560,256]{1,0:T(8,128)S(1)} %bitcast_add_fusion, f32[1280,2560]{1,0:T(8,128)} %param.28), kind=kOutput, calls=%fused_computation.21 | convolution fusion | flops 10066329600 | bytes 17039360 | tf_op jit(solution)/shard_map/dot_general | solution.py:116
  431.1 54.7 %all-reduce.6.cloned.1.call-done = f32[1280,256]{0,1:T(8,128)} async-done(((f32[1280,256]{0,1:T(8,128)}), f32[1280,256]{0,1:T(8,128)}) %all-reduce.6.cloned.1.call-update) | async-done | bytes 1310736 | tf_op jit(solution)/shard_map/psum | solution.py:27
  485.8 15.9 %convolution_bitcast_fusion = f32[2560,256]{0,1:T(8,128)} fusion(f32[1280,256]{0,1:T(8,128)} %all-reduce.6.cloned.1.call-done, f32[2560,1280]{1,0:T(8,128)} %param.29), kind=kOutput, calls=%fused_computation.13 | convolution fusion | flops 10066329600 | bytes 17039360 | tf_op jit(solution)/shard_map/dot_general | solution.py:124
  501.8 185.6 %all-gather.13.cloned.1.call-done = f32[20480,256]{0,1:T(8,128)} async-done(((f32[2560,256]{0,1:T(8,128)}), f32[20480,256]{0,1:T(8,128)}) %all-gather.13.cloned.1.call-update) | async-done | bytes 20971536 | tf_op jit(solution)/shard_map/all_gather | solution.py:11
  687.3 23.4 %copy.98 = f32[32,8,8,2560]{3,2,1,0:T(8,128)S(1)} copy(f32[32,8,8,2560]{3,1,2,0:T(8,128)} %bitcast.125) | data formatting | bytes 41943040
  710.7 7.1 bitcast_reduce_fusion
  717.8 2.2 copy.72
  720.1 4.4 fusion.12
  724.5 0.6 copy.74
  725.1 1.5 copy-done.2
  726.6 8.0 convolution_bitcast_fusion.5
  734.7 50.8 %all-reduce.8.cloned.1.call-done = f32[2,512,256]{1,2,0:T(8,128)} async-done(((f32[2,512,256]{1,2,0:T(8,128)}), f32[2,512,256]{1,2,0:T(8,128)}) %all-reduce.8.cloned.1.call-update) | async-done | bytes 1048592 | tf_op jit(solution)/shard_map/psum | solution.py:27
  785.5 7.5 convolution_bitcast_fusion.3
  793.0 2.9 copy.76
  795.9 0.3 reduce-scatter.9.cloned.1.call-start
  796.2 0.6 dynamic_slice.16
  796.8 0.1 dynamic-slice_bitcast_fusion
  796.8 0.6 iota_compare_fusion.1
  797.5 0.1 broadcast_compare_fusion.1
  797.6 149.6 %all-gather.15.cloned.1.call-done = f32[16,1024,256]{2,1,0:T(8,128)} async-done(((f32[2,1024,256]{2,1,0:T(8,128)}), f32[16,1024,256]{2,1,0:T(8,128)}) %all-gather.15.cloned.1.call-update) | async-done | bytes 16777232 | tf_op jit(solution)/shard_map/all_gather | solution.py:11
  947.1 8.5 reduce_sum.32
  955.6 2.8 copy.79
  958.4 1.9 fusion.39
  960.4 0.1 copy.81
  960.5 0.1 copy-done.4
  960.6 8.4 fusion.21
  969.0 0.3 reduce-scatter.11.cloned.1.call-start
  969.3 33.2 %reduce-scatter.9.cloned.1.call-done = f32[512,256]{0,1:T(8,128)} async-done(((f32[2048,256]{0,1:T(8,128)}), f32[512,256]{0,1:T(8,128)}) %reduce-scatter.9.cloned.1.call-update) | async-done | bytes 524304 | tf_op jit(solution)/shard_map/reduce_scatter | solution.py:16
  1002.5 7.4 fusion.24
  1009.9 35.4 %reduce-scatter.11.cloned.1.call-done = f32[512,256]{0,1:T(8,128)} async-done(((f32[2048,256]{0,1:T(8,128)}), f32[512,256]{0,1:T(8,128)}) %reduce-scatter.11.cloned.1.call-update) | async-done | bytes 524304 | tf_op jit(solution)/shard_map/reduce_scatter | solution.py:16
  1045.2 1.1 multiply_bitcast_fusion
  1046.3 1.0 copy.82
  (38 shorter events, 0.6 us)
Async XLA Ops:
  7.2 95.4 %copy-start = (s32[8,16]{1,0:T(8,128)S(1)}, s32[8,16]{1,0:T(8,128)}, u32[]{:S(2)}) copy-start(s32[8,16]{1,0:T(8,128)} %param.32) | copy-start | bytes 1540
  7.2 50.6 %reduce-scatter.5.cloned.1.call-start = ((), (), s32[]{:S(2)}) async-start(), calls=%async_computation.4 | async-start | bytes 2621440 | tf_op jit(solution)/shard_map/reduce_scatter | solution.py:16
  19.7 80.7 %reduce-scatter.7.cloned.1.call-start = ((), (), s32[]{:S(2)}) async-start(), calls=%async_computation.5 | async-start | bytes 2621440 | tf_op jit(solution)/shard_map/reduce_scatter | solution.py:16
  65.1 37.7 %copy-start.10 = (s32[8]{0:T(128)S(1)}, s32[8]{0:T(128)}, u32[]{:S(2)}) copy-start(s32[8]{0:T(128)} %param.30) | copy-start | bytes 100
  65.1 84.4 %all-gather.9.cloned.1.call-start = ((), (), s32[]{:S(2)}) async-start(), calls=%async_computation.11 | async-start | bytes 4718592 | tf_op jit(solution)/shard_map/all_gather | solution.py:91
  102.3 129.5 %all-reduce.4.cloned.1.call-start = ((), (), s32[]{:S(2)}) async-start(), calls=%async_computation.6 | async-start | bytes 2097152 | tf_op jit(solution)/shard_map/psum | solution.py:27
  168.2 2.1 copy-start.1
  168.2 3.1 copy-start.7
  168.3 4.2 copy-start.3
  180.4 211.1 %all-gather.11.cloned.1.call-start = ((), (), s32[]{:S(2)}) async-start(), calls=%async_computation.12 | async-start | bytes 18874368 | tf_op jit(solution)/shard_map/all_gather | solution.py:11
  238.4 1.9 copy-start.9
  240.2 245.6 %all-reduce.6.cloned.1.call-start = ((), (), s32[]{:S(2)}) async-start(), calls=%async_computation.7 | async-start | bytes 2621440 | tf_op jit(solution)/shard_map/psum | solution.py:27
  403.1 1.7 copy-start.6
  431.1 256.2 %all-gather.13.cloned.1.call-start = ((), (), s32[]{:S(2)}) async-start(), calls=%async_computation.13 | async-start | bytes 23592960 | tf_op jit(solution)/shard_map/all_gather | solution.py:11
  501.7 283.8 %all-reduce.8.cloned.1.call-start = ((), (), s32[]{:S(2)}) async-start(), calls=%async_computation.8 | async-start | bytes 2097152 | tf_op jit(solution)/shard_map/psum | solution.py:27
  724.4 2.2 copy-start.2
  726.6 58.9 %copy-start.5 = (f32[2,512,256]{1,2,0:T(8,128)S(1)}, f32[2,512,256]{1,2,0:T(8,128)}, u32[]{:S(2)}) copy-start(f32[2,512,256]{1,2,0:T(8,128)} %all-reduce.4.cloned.1.call-done) | copy-start | bytes 3145732
  734.7 212.4 %all-gather.15.cloned.1.call-start = ((), (), s32[]{:S(2)}) async-start(), calls=%async_computation.14 | async-start | bytes 18874368 | tf_op jit(solution)/shard_map/all_gather | solution.py:11
  795.9 206.6 %reduce-scatter.9.cloned.1.call-start = ((), (), s32[]{:S(2)}) async-start(), calls=%async_computation.9 | async-start | bytes 2621440 | tf_op jit(solution)/shard_map/reduce_scatter | solution.py:16
  958.4 2.2 copy-start.4
  960.6 41.9 %copy-start.8 = (f32[512,256]{0,1:T(8,128)S(1)}, f32[512,256]{0,1:T(8,128)}, u32[]{:S(2)}) copy-start(f32[512,256]{0,1:T(8,128)} %reduce-scatter.5.cloned.1.call-done) | copy-start | bytes 1572868
  969.0 76.3 %reduce-scatter.11.cloned.1.call-start = ((), (), s32[]{:S(2)}) async-start(), calls=%async_computation.10 | async-start | bytes 2621440 | tf_op jit(solution)/shard_map/reduce_scatter | solution.py:16
Sparse Core Ops, SparseCore 0:
  19.8 37.9 reduce-scatter.4
  65.2 35.1 reduce-scatter.6
  102.6 46.8 all-gather.8
  180.5 51.2 all-reduce.3
  240.4 151.0 all-gather.10
  431.2 54.5 all-reduce.5
  501.8 185.4 all-gather.12
  734.8 50.6 all-reduce.7
  796.0 151.0 all-gather.14
  969.1 33.3 reduce-scatter.8
  1010.0 35.1 reduce-scatter.10
